TPU v7x, 32 devices: a whole 2x2x4 slice. The times are simulated.
32 devices in a mesh: band: 4 (over y, x), col: 8 (over z, core).
Axes of the slice: x: 2, y: 2, z: 4, core: 2. Of those that a mesh axis runs over, the one named last changes fastest.
Arguments:
- control: bfloat16 [4, 640, 320, 137], P('band', 'col'), may hold values from -6 to 6
- vertical_root: bfloat16 [3, 137, 128], replicated, may hold values from -0.5 to 0.5
- legendre: bfloat16 [320, 320, 320], P('col'), may hold values from -0.3125 to 0.3125
- band_filter: float32 [3, 320], replicated, may hold values from 0.3 to 1.7
- row_plan: int32 [4, 2], P('band'), may hold values from 0 to 16, as said below
- wave_order: int32 [320], replicated, may hold values from 0 to 319, each once
- lat_points: int32 [320], P('col'), may hold values from 16 to 640, as said below
- support: int32 [3, 2], replicated, may hold values from 0 to 320, as said below
Outputs:
- spectrum: float32 [320, 320, 2, 128], P('col', 'band')
Inputs may be any that keep to these rules, and one draw needn't show every extreme that they name: `row_plan`: column 0 is the band of the row: 2 (coarsest) on max(1, 0) rows, 1 on max(1, 0) rows, 0 (finest) on the rest, rows drawn at random. Column 1 is the row's first output level; some row starts at 0 and some at 16. `lat_points`: counts rise with the distance from the nearest pole, apart from a jitter of up to 7 points between neighbouring latitudes; latitudes near the equator have all 640 points. `support`: row b is band b; band 0 ends at 320, band 2 starts at 0; every band's range is non-empty and the ranges of neighbouring bands intersect.
All inputs are finite; a program needn't handle non-finite values.
Results may differ from a plain program's by a relative error of at most 0.012.
Values may be sent and summed in bfloat16 or wider, within the bound.
A program may use at most 128 MiB of HBM per device.

v0:
```python
import math

import jax
import jax.numpy as jnp
from jax import lax
from jax.sharding import PartitionSpec as P

LVR = 112
LEVW = 128


def dft_rows(points, wave_list, lon_count):
    lon_index = jnp.arange(lon_count, dtype=jnp.int32)[:, None]
    phase_step = wave_list[None, :] * lon_index % points
    angles = 2.0 * math.pi * phase_step.astype(jnp.float32) / points.astype(jnp.float32)
    live_mask = (lon_index < points).astype(jnp.float32) / jnp.sqrt(points.astype(jnp.float32))
    return (jnp.concatenate([jnp.cos(angles), -jnp.sin(angles)], axis=1) * live_mask).astype(
        jnp.bfloat16
    )


def per_device(
    control, vertical_root, legendre, band_filter, row_plan, wave_order, lat_points, support
):
    band_id = row_plan[0, 0]
    level_start = row_plan[0, 1]
    root_band = lax.dynamic_index_in_dim(vertical_root, band_id, 0, keepdims=False)
    root_block = lax.dynamic_slice_in_dim(root_band, level_start, LVR, 1)
    columns = control[0]
    rooted = jnp.dot(columns, root_block, preferred_element_type=jnp.float32).astype(jnp.bfloat16)
    grid_field = lax.all_to_all(rooted, "col", split_axis=1, concat_axis=0, tiled=True)
    lon_count = grid_field.shape[0]
    lat_local = grid_field.shape[1]
    mode_count = wave_order.shape[0]

    def one_lat(lat_index):
        weights = dft_rows(lat_points[lat_index], wave_order, lon_count)
        column = lax.dynamic_index_in_dim(grid_field, lat_index, 1, keepdims=False)
        return lax.dot_general(
            weights, column, (((0,), (0,)), ((), ())), preferred_element_type=jnp.float32
        ).astype(jnp.bfloat16)

    fourier = lax.map(one_lat, jnp.arange(lat_local, dtype=jnp.int32)).reshape(
        lat_local, 2, mode_count, LVR
    )
    slot_count = legendre.shape[0]
    degree_count = legendre.shape[2]
    owned_waves = lax.dynamic_slice_in_dim(
        wave_order, lax.axis_index("col") * slot_count, slot_count
    )
    degree = jnp.arange(degree_count, dtype=jnp.int32)
    bounds = lax.dynamic_index_in_dim(support, band_id, 0, keepdims=False)
    filter_row = lax.dynamic_index_in_dim(band_filter, band_id, 0, keepdims=False)
    window = filter_row * ((degree >= bounds[0]) & (degree < bounds[1])).astype(jnp.float32)
    spectral_weight = (degree[None, :] >= owned_waves[:, None]).astype(jnp.float32) * window[
        None, :
    ]
    spectral_owned = lax.all_to_all(fourier, "col", split_axis=2, concat_axis=0, tiled=True)
    spectral = jnp.einsum(
        "xpsl,sxn->snpl", spectral_owned, legendre, preferred_element_type=jnp.float32
    )
    contribution = spectral * spectral_weight[:, :, None, None]
    placed = jnp.zeros((slot_count, degree_count, 2, LEVW), jnp.float32)
    placed = lax.dynamic_update_slice_in_dim(placed, contribution, level_start, 3)
    return lax.psum_scatter(
        placed.astype(jnp.bfloat16), "band", scatter_dimension=1, tiled=True
    ).astype(jnp.float32)


def solution(mesh):
    in_specs = (
        P("band", "col", None, None),
        P(),
        P("col", None, None),
        P(),
        P("band", None),
        P(),
        P("col"),
        P(),
    )
    out_specs = P("col", "band", None, None)
    return jax.shard_map(
        per_device, mesh=mesh, in_specs=in_specs, out_specs=out_specs, check_vma=False
    )
```

profile of v0, /device:TPU:0, one launch (start us, length us, event | category | flops | bytes accessed | tf_op | source)
XLA Modules:
  0.0 1437.9 jit_solution(14085990716266382399)
XLA Ops:
  34.0 144.6 %all-to-all-done = bf16[80,320,112]{2,0,1:T(8,128)(2,1)} async-done(((bf16[80,320,112]{2,0,1:T(8,128)(2,1)}), bf16[80,320,112]{2,0,1:T(8,128)(2,1)}, u32[]{:S(2)}, u32[]{:S(2)}) %all-to-all-start) | async-done | bytes 5734432 | tf_op jit(solution)/shard_map/all_to_all | solution.py:31
  196.4 818.6 %while.10 = (s32[]{:T(128)}, bf16[40,640,112]{1,2,0:T(8,128)(2,1)}, s32[320]{0:T(512)S(1)}, s32[40]{0:T(128)S(1)}, s32[40]{0:T(128)S(1)}, /*index=5*/bf16[640,40...) while((s32[]{:T(128)}, bf16[40,640,112]{1,2,0:T(8,128)(2,1)}, s32[320]{0:T(512)S(1)}, s32[40]{0:T(128)S(1)}, ...), condition=%wide.region_1.2_spmd, body=%wide.region_0.1_spmd.sunk | while | flops 95509768 | bytes 3570151 | solution.py:43
  202.0 13.0 fusion.41
  222.4 13.0 fusion.41
  242.9 13.0 fusion.41
  263.3 13.0 fusion.41
  283.8 13.0 fusion.41
  304.2 13.0 fusion.41
  324.7 13.0 fusion.41
  365.6 13.0 fusion.41
  386.1 13.0 fusion.41
  406.5 13.0 fusion.41
  426.9 13.0 fusion.41
  447.4 13.0 fusion.41
  467.9 13.0 fusion.41
  529.2 13.0 fusion.41
  590.6 13.0 fusion.41
  631.5 13.0 fusion.41
  652.0 13.0 fusion.41
  713.3 13.0 fusion.41
  774.7 13.0 fusion.41
  795.1 13.0 fusion.41
  836.0 13.0 fusion.41
  856.5 13.0 fusion.41
  877.0 13.0 fusion.41
  897.4 13.0 fusion.41
  958.8 13.0 fusion.41
  979.2 13.0 fusion.41
  1023.5 28.3 %copy.31 = bf16[40,2,320,112]{3,1,0,2:T(2,128)(2,1)} copy(bf16[40,2,320,112]{3,2,1,0:T(8,128)(2,1)} %bitcast.47) | data formatting | bytes 11468800 | tf_op jit(solution)/shard_map/reshape | solution.py:43
  1059.5 141.8 %all-to-all-done.1 = bf16[40,2,320,112]{3,1,0,2:T(2,128)(2,1)} async-done(((bf16[40,2,320,112]{3,1,0,2:T(2,128)(2,1)}), bf16[40,2,320,112]{3,1,0,2:T(2,128)(2,1)}, u32[]{:S(2)}, u32[]{:S(2)}) %all-to-all-start.1) | async-done | bytes 5734432 | tf_op jit(solution)/shard_map/all_to_all | solution.py:58
  1232.8 122.6 %dynamic_update_slice.7 = bf16[40,320,2,128]{3,0,2,1:T(8,128)(2,1)} dynamic-update-slice(bf16[40,320,2,128]{3,0,2,1:T(8,128)(2,1)} %broadcast_in_dim.10, bf16[40,320,2,112]{3,0,2,1:T(8,128)(2,1)} %copy.35, s32[]{:T(128)} %constant.65.clone.1, s32[]{:T(128)} %constant.65.clone.1, s32[]{:T(128)} %constant.65.clone.1, s32[]{:T(128)S(6)} %select_n.35) | dynamic-update-slice | bytes 11468804 | tf_op jit(solution)/shard_map/dynamic_update_slice | solution.py:64
  1355.5 70.3 %reduce-scatter.2.cloned.1.call-done = bf16[40,80,2,128]{3,0,2,1:T(8,128)(2,1)} async-done(((bf16[40,320,2,128]{3,0,2,1:T(8,128)(2,1)}), bf16[40,80,2,128]{3,0,2,1:T(8,128)(2,1)}) %reduce-scatter.2.cloned.1.call-update) | async-done | bytes 1638416 | tf_op jit(solution)/shard_map/reduce_scatter | solution.py:65
  (207 shorter events, 433.9 us)
Async XLA Ops:
  6.5 5.2 copy-start
  27.6 151.0 %all-to-all-start = ((bf16[80,320,112]{2,0,1:T(8,128)(2,1)}), bf16[80,320,112]{2,0,1:T(8,128)(2,1)}, u32[]{:S(2)}, u32[]{:S(2)}) async-start(bf16[80,320,112]{2,0,1:T(8,128)(2,1)} %copy.27), calls=%async_computation | async-start | bytes 13107200 | tf_op jit(solution)/shard_map/all_to_all | solution.py:31
  185.9 10.5 copy-start.2
  185.9 10.5 copy-start.4
  1051.8 5.1 copy-start.3
  1051.8 149.5 %all-to-all-start.1 = ((bf16[40,2,320,112]{3,1,0,2:T(2,128)(2,1)}), bf16[40,2,320,112]{3,1,0,2:T(2,128)(2,1)}, u32[]{:S(2)}, u32[]{:S(2)}) async-start(bf16[40,2,320,112]{3,1,0,2:T(2,128)(2,1)} %copy.31), calls=%async_computation.1 | async-start | bytes 13107200 | tf_op jit(solution)/shard_map/all_to_all | solution.py:58
  1056.8 369.1 %reduce-scatter.2.cloned.1.call-start = ((), (), s32[]{:S(2)}) async-start(), calls=%async_computation.3 | async-start | bytes 8192000 | tf_op jit(solution)/shard_map/reduce_scatter | solution.py:65
  1232.8 198.0 %copy-start.1 = (bf16[3,137,128]{2,1,0:T(8,128)(2,1)S(1)}, bf16[3,137,128]{2,1,0:T(8,128)(2,1)}, u32[]{:S(2)}) copy-start(bf16[3,137,128]{2,1,0:T(8,128)(2,1)} %param.11) | copy-start | bytes 315652
Sparse Core Ops, SparseCore 0:
  1355.6 70.1 reduce-scatter.1
where the time goes:
time: 1450 us; the launch traced here: 1440 us
  other arithmetic  545 us (38%)
  waiting for transfers between devices  357 us (25%)
  local copies, waits for them, and re-layouts  261 us (18%)
  loops' own time  141 us (10%)
  matrix products  106 us (7%)
  between operations  17.5 us (1%)
    cos x40, other arithmetic, dft_rows(): jnp.cos(angles)  520 us
    all_to_all x1, waiting for transfers between devices, per_device(): lax.all_to_all(rooted, 'col', split_axis=1, concat_axis=0, tiled=True)  145 us
    all_to_all x1, waiting for transfers between devices, per_device(): lax.all_to_all(fourier, 'col', split_axis=2, concat_axis=0, tiled=True)  142 us
    another operation x1, loops' own time, per_device(): lax.map(one_lat, jnp.arange(lat_local, dtype=jnp.int32))  141 us
    dynamic_update_slice x1, local copies, waits for them, and re-layouts, per_device(): lax.dynamic_update_slice_in_dim(placed, contribution, level_start, 3)  123 us
    dot_general x40, matrix products, one_lat(): lax.dot_general(weights, column, (((0,), (0,)), ((), ())), preferred_elem...  87.6 us
    reduce_scatter x1, waiting for transfers between devices, per_device(): lax.psum_scatter(placed.astype(jnp.bfloat16), 'band', scatter_dimension=1...  70.3 us
  transfers between devices with their start and end apart: 3, of which 3 were waited for; matrix products, arithmetic and copies ran while one was open for 0% of the time, Pallas kernels for 0%

commit v1 on v0

v1 whole, which is shorter than its diff:
```python
import math

import jax
import jax.numpy as jnp
from jax import lax
from jax.experimental import pallas as pl
from jax.experimental.pallas import tpu as pltpu
from jax.sharding import PartitionSpec as P

LVR = 112
CHUNKS = 2


def weights_kernel(points_ref, wave_ref, part_ref, out_ref):
    count = jnp.full((1, 1), points_ref[pl.program_id(0)], jnp.int32).astype(jnp.float32)
    _, cols, lons = out_ref.shape
    tile = 8 if cols % 16 else 16
    lon = lax.broadcasted_iota(jnp.int32, (1, lons), 1).astype(jnp.float32)
    inverse = 1.0 / count
    scale = jnp.where(lon < count, lax.rsqrt(count), 0.0)

    def rows(k, carry):
        at = pl.ds(pl.multiple_of(k * tile, tile), tile)
        turns = (4.0 * wave_ref[at, :]) * lon
        quarter = jnp.round(turns * inverse)
        theta = (turns - quarter * count) * ((0.5 * math.pi) * inverse)
        square = theta * theta
        quadrant = quarter.astype(jnp.int32) + part_ref[at, :]
        odd = (quadrant & 1) == 1
        value = jnp.where(odd, 1.0 / 362880.0, 1.0 / 40320.0)
        value = value * square + jnp.where(odd, -1.0 / 5040.0, -1.0 / 720.0)
        value = value * square + jnp.where(odd, 1.0 / 120.0, 1.0 / 24.0)
        value = value * square + jnp.where(odd, -1.0 / 6.0, -0.5)
        value = value * square + 1.0
        value = value * jnp.where(odd, theta, 1.0)
        sign = jnp.where(((quadrant + 1) & 2) == 0, scale, -scale)
        out_ref[0, at, :] = (value * sign).astype(jnp.bfloat16)
        return carry

    lax.fori_loop(0, cols // tile, rows, 0)


def dft_weights(points, waves, lon_count):
    owners, slots = waves.shape
    lats = points.shape[0]
    cols = owners * 2 * slots
    shape = (owners, 2, slots)
    wave = jnp.broadcast_to(waves.astype(jnp.float32)[:, None], shape).reshape(cols, 1)
    part = jnp.broadcast_to(
        jnp.arange(2, dtype=jnp.int32)[None, :, None], shape
    ).reshape(cols, 1)
    return pl.pallas_call(
        weights_kernel,
        grid_spec=pltpu.PrefetchScalarGridSpec(
            num_scalar_prefetch=1,
            grid=(lats,),
            in_specs=[
                pl.BlockSpec((cols, 1), lambda i, p: (0, 0)),
                pl.BlockSpec((cols, 1), lambda i, p: (0, 0)),
            ],
            out_specs=pl.BlockSpec((1, cols, lon_count), lambda i, p: (i, 0, 0)),
        ),
        out_shape=jax.ShapeDtypeStruct((lats, cols, lon_count), jnp.bfloat16),
        cost_estimate=pl.CostEstimate(
            flops=25 * lats * cols * lon_count,
            bytes_accessed=2 * lats * cols * lon_count,
            transcendentals=0,
        ),
        name="weights",
    )(points, wave, part)


def dft_kernel(weight_ref, grid_ref, out_ref):
    lons = grid_ref.shape[0] * grid_ref.shape[2]
    column = grid_ref[:, 0].reshape(lons, grid_ref.shape[3])
    result = jnp.dot(weight_ref[0], column, preferred_element_type=jnp.float32)
    owners, _, rows, levels = out_ref.shape
    out_ref[:, 0] = result.astype(jnp.bfloat16).reshape(owners, rows, levels)


def dft(weights, grid_field, owners):
    lats, cols, lons = weights.shape
    ranks, _, lon_local, levels = grid_field.shape
    rows = cols // owners
    return pl.pallas_call(
        dft_kernel,
        grid=(lats,),
        in_specs=[
            pl.BlockSpec((1, cols, lons), lambda i: (i, 0, 0)),
            pl.BlockSpec((ranks, 1, lon_local, levels), lambda i: (0, i, 0, 0)),
        ],
        out_specs=pl.BlockSpec((owners, 1, rows, levels), lambda i: (0, i, 0, 0)),
        out_shape=jax.ShapeDtypeStruct((owners, lats, rows, levels), jnp.bfloat16),
        cost_estimate=pl.CostEstimate(
            flops=2 * lats * cols * lons * levels,
            bytes_accessed=2 * lats * (cols * lons + (cols + lons) * levels),
            transcendentals=0,
        ),
        name="dft",
    )(weights, grid_field)


def per_device(
    control, vertical_root, legendre, band_filter, row_plan, wave_order, lat_points, support
):
    owners = lax.axis_size("col")
    band_id = row_plan[0, 0]
    level_start = row_plan[0, 1]
    root_band = lax.dynamic_index_in_dim(vertical_root, band_id, 0, keepdims=False)
    level = jnp.arange(root_band.shape[1], dtype=jnp.int32)
    inside = (level >= level_start) & (level < level_start + LVR)
    root_block = jnp.where(inside[None, :], root_band, jnp.zeros_like(root_band))
    columns = control[0]
    lon_local, lat_count, _ = columns.shape
    rooted = jnp.einsum(
        "jik,kl->ijl", columns, root_block, preferred_element_type=jnp.float32
    ).astype(jnp.bfloat16)
    rooted = rooted.reshape(owners, lat_count // owners, lon_local, -1)
    grid_field = lax.all_to_all(rooted, "col", split_axis=0, concat_axis=0, tiled=True)
    lon_count = lon_local * owners
    lat_local = lat_count // owners

    slot_count = legendre.shape[0]
    degree_count = legendre.shape[2]
    step = slot_count // CHUNKS
    waves = wave_order.reshape(owners, CHUNKS, step)
    owned_waves = lax.dynamic_index_in_dim(waves, lax.axis_index("col"), 0, keepdims=False)
    degree = jnp.arange(degree_count, dtype=jnp.int32)
    bounds = lax.dynamic_index_in_dim(support, band_id, 0, keepdims=False)
    filter_row = lax.dynamic_index_in_dim(band_filter, band_id, 0, keepdims=False)
    window = filter_row * ((degree >= bounds[0]) & (degree < bounds[1])).astype(jnp.float32)

    weights = [
        dft_weights(lat_points, waves[:, c], lon_count)
        for c in range(CHUNKS)
    ]
    outputs = []
    for c in range(CHUNKS):
        fourier = dft(weights[c], grid_field, owners)
        owned = lax.all_to_all(fourier, "col", split_axis=0, concat_axis=0, tiled=True)
        owned = owned.reshape(lat_count, 2, step, owned.shape[3])
        spectral = jnp.einsum(
            "xpsl,sxn->snpl",
            owned,
            lax.slice_in_dim(legendre, c * step, (c + 1) * step, axis=0),
            preferred_element_type=jnp.float32,
        )
        spectral_weight = (degree[None, :] >= owned_waves[c][:, None]).astype(
            jnp.float32
        ) * window[None, :]
        contribution = (spectral * spectral_weight[:, :, None, None]).astype(jnp.bfloat16)
        outputs.append(
            lax.psum_scatter(contribution, "band", scatter_dimension=1, tiled=True)
        )
    return jnp.concatenate(outputs, axis=0).astype(jnp.float32)


def solution(mesh):
    in_specs = (
        P("band", "col", None, None),
        P(),
        P("col", None, None),
        P(),
        P("band", None),
        P(),
        P("col"),
        P(),
    )
    out_specs = P("col", "band", None, None)
    return jax.shard_map(
        per_device, mesh=mesh, in_specs=in_specs, out_specs=out_specs, check_vma=False
    )
```

time: 1450 us -> 490 us (0.34)
  other arithmetic: 545 us -> 4.31 us
  waiting for transfers between devices: 357 us -> 90.6 us
  Pallas kernels: 0 us -> 252 us
  local copies, waits for them, and re-layouts: 261 us -> 16.3 us
  loops' own time: 141 us -> 0 us
  matrix products: 106 us -> 19.8 us
  blocking collectives: 0 us -> 79.1 us
    cos x40 -> x0, other arithmetic: 520 us -> none  [dft_rows(): jnp.cos(angles)]
    pallas_call x0 -> x4, Pallas kernels: none -> 252 us  [the longest x2 193 us: dft_weights(): pl.pallas_call(weights_kernel, grid_spec=pltpu.PrefetchScalarGridSpec(num...]
    all_to_all x2, waiting for transfers between devices: 286 us -> 46.5 us  [the longest x1 46.5 us: per_device(): lax.all_to_all(rooted, 'col', split_axis=0, concat_axis=0, tiled=True)]
    another operation x1 -> x0, loops' own time: 141 us -> none  [per_device(): lax.map(one_lat, jnp.arange(lat_local, dtype=jnp.int32))]
    dynamic_update_slice x1 -> x0, local copies, waits for them, and re-layouts: 123 us -> none  [per_device(): lax.dynamic_update_slice_in_dim(placed, contribution, level_start, 3)]
    dot_general x42 -> x3, matrix products: 106 us -> 19.8 us  [the longest x2 10.9 us: per_device(): jnp.einsum('xpsl,sxn->snpl', owned, lax.slice_in_dim(legendre, c * step,...]
    all_to_all x0 -> x1, blocking collectives: none -> 79.1 us  [per_device(): lax.all_to_all(fourier, 'col', split_axis=0, concat_axis=0, tiled=True)]
    dynamic_slice x81 -> x1, local copies, waits for them, and re-layouts: 47.4 us -> 0.01 us  [per_device(): lax.dynamic_index_in_dim(waves, lax.axis_index('col'), 0, keepdims=False)]
  transfers between devices with their start and end apart: 3 -> 4, of which waited for: 3 -> 2; matrix products, arithmetic and copies ran while one was open for 0% -> 2% of each run, Pallas kernels for 0% -> 46%
where the time goes in v1:
time: 490 us; the launch traced here: 488 us
  Pallas kernels  252 us (51%)
  waiting for transfers between devices  90.6 us (18%)
  blocking collectives  79.1 us (16%)
  matrix products  19.8 us (4%)
  local copies, waits for them, and re-layouts  16.3 us (3%)
  between operations  16 us (3%)
  starting transfers between devices  10.4 us (2%)
    pallas_call x2, Pallas kernels, dft_weights(): pl.pallas_call(weights_kernel, grid_spec=pltpu.PrefetchScalarGridSpec(num...  193 us
    all_to_all x1, blocking collectives, per_device(): lax.all_to_all(fourier, 'col', split_axis=0, concat_axis=0, tiled=True)  79.1 us
    pallas_call x2, Pallas kernels, dft(): pl.pallas_call(dft_kernel, grid=(lats,), in_specs=[pl.BlockSpec((1, cols,...  58.7 us
    all_to_all x1, waiting for transfers between devices, per_device(): lax.all_to_all(rooted, 'col', split_axis=0, concat_axis=0, tiled=True)  46.5 us
    reduce_scatter x2, waiting for transfers between devices, per_device(): lax.psum_scatter(contribution, 'band', scatter_dimension=1, tiled=True)  44 us
    dot_general x2, matrix products, per_device(): jnp.einsum('xpsl,sxn->snpl', owned, lax.slice_in_dim(legendre, c * step,...  10.9 us
  transfers between devices with their start and end apart: 4, of which 2 were waited for; matrix products, arithmetic and copies ran while one was open for 2% of the time, Pallas kernels for 46%

profile of v1, /device:TPU:0, one launch (start us, length us, event | category | flops | bytes accessed | tf_op | source)
XLA Modules:
  0.0 488.1 jit_solution(9808693152272397311)
XLA Ops:
  6.5 1.3 fusion.37
  9.8 0.7 compare_and_fusion
  11.0 8.9 %fusion.5 = bf16[320,80,128]{2,0,1:T(8,128)(2,1)S(1)} fusion(bf16[80,320,137]{1,0,2:T(8,128)(2,1)} %bitcast.41, bf16[3,137,128]{2,1,0:T(8,128)(2,1)} %param.9, s32[]{:T(128)S(6)} %select_n.19, pred[128]{0:T(512)(128)(4,1)S(1)} %compare_and_fusion), kind=kOutput, calls=%fused_computation.5 | convolution fusion | flops 901137536 | bytes 15007876 | tf_op jit(solution)/shard_map/jik,kl->ijl/dot_general | solution.py:115
  20.0 6.9 %copy.19 = bf16[320,80,128]{2,1,0:T(8,128)(2,1)} copy(bf16[320,80,128]{2,0,1:T(8,128)(2,1)S(1)} %fusion.5) | data formatting | bytes 13107200 | tf_op jit(solution)/shard_map/convert_element_type | solution.py:117
  26.9 6.5 %all-to-all-start = ((bf16[8,40,80,128]{3,2,1,0:T(8,128)(2,1)}), bf16[8,40,80,128]{3,2,1,0:T(8,128)(2,1)}, u32[]{:S(2)}, u32[]{:S(2)}) async-start(bf16[8,40,80,128]{3,2,1,0:T(8,128)(2,1)} %bitcast.40), calls=%async_computation | async-start | bytes 13107200 | tf_op jit(solution)/shard_map/all_to_all | solution.py:119
  33.4 0.1 reshape.138
  33.5 0.8 reshape.150.part_ref
  34.3 0.8 reshape.149.wave_ref
  35.1 96.4 %weights.3.weight_ref = bf16[40,320,640]{2,1,0:T(8,128)(2,1)} custom-call(s32[40]{0:T(128)} %points_ref.3, f32[320,1]{1,0:T(8,128)} %reshape.149.wave_ref, s32[320,1]{1,0:T(8,128)} %reshape.150.part_ref), custom_call_target="tpu_custom_call" | custom-call | flops 204800000 | bytes 16384000 | tf_op jit(solution)/shard_map/weights/pallas_call | solution.py:52
  131.5 46.5 %all-to-all-done.grid_ref = bf16[8,40,80,128]{3,2,1,0:T(8,128)(2,1)} async-done(((bf16[8,40,80,128]{3,2,1,0:T(8,128)(2,1)}), bf16[8,40,80,128]{3,2,1,0:T(8,128)(2,1)}, u32[]{:S(2)}, u32[]{:S(2)}) %all-to-all-start) | async-done | bytes 6553632 | tf_op jit(solution)/shard_map/all_to_all | solution.py:119
  178.0 29.2 %dft.3 = bf16[8,40,40,128]{3,2,1,0:T(8,128)(2,1)} custom-call(bf16[40,320,640]{2,1,0:T(8,128)(2,1)} %weights.3.weight_ref, bf16[8,40,80,128]{3,2,1,0:T(8,128)(2,1)} %all-to-all-done.grid_ref), custom_call_target="tpu_custom_call" | custom-call | flops 2097152000 | bytes 26214400 | tf_op jit(solution)/shard_map/dft/pallas_call | solution.py:85
  207.2 3.7 all-to-all-start.2
  210.9 0.2 reduce-scatter.5.cloned.1.call-start
  211.1 0.8 reshape.148.wave_ref
  211.9 0.1 constant_dynamic-slice_fusion
  212.0 0.6 fusion.36
  212.5 2.0 fusion.33
  214.5 96.4 %weights.2.weight_ref = bf16[40,320,640]{2,1,0:T(8,128)(2,1)} custom-call(s32[40]{0:T(128)} %points_ref.3, f32[320,1]{1,0:T(8,128)} %reshape.148.wave_ref, s32[320,1]{1,0:T(8,128)} %reshape.150.part_ref), custom_call_target="tpu_custom_call" | custom-call | flops 204800000 | bytes 16384000 | tf_op jit(solution)/shard_map/weights/pallas_call | solution.py:52
  310.9 0.1 fusion.29
  311.0 0.8 copy.25
  311.8 5.4 %fusion.15 = bf16[20,320,2,128]{3,1,2,0:T(8,128)(2,1)} fusion(f32[20,320]{1,0:T(8,128)S(1)} %get-tuple-element.8, bf16[320,2,20,128]{3,0,2,1:T(8,128)(2,1)S(1)} %bitcast.43, bf16[40,320,320]{2,1,0:T(8,128)(2,1)} %param.10), kind=kOutput, calls=%fused_computation.13 | convolution fusion | flops 1051852800 | bytes 11494400 | tf_op jit(solution)/shard_map/xpsl,sxn->snpl/dot_general | solution.py:142
  317.3 0.0 reduce-scatter.5.cloned.1.call-update
  317.3 0.0 reduce-scatter.3.cloned.1.call-start
  317.3 29.5 %dft.2 = bf16[8,40,40,128]{3,2,1,0:T(8,128)(2,1)} custom-call(bf16[40,320,640]{2,1,0:T(8,128)(2,1)} %weights.2.weight_ref, bf16[8,40,80,128]{3,2,1,0:T(8,128)(2,1)} %all-to-all-done.grid_ref), custom_call_target="tpu_custom_call" | custom-call | flops 2097152000 | bytes 26214400 | tf_op jit(solution)/shard_map/dft/pallas_call | solution.py:85
  346.8 79.1 %all_to_all.15 = bf16[8,40,40,128]{3,2,1,0:T(8,128)(2,1)S(1)} all-to-all(bf16[8,40,40,128]{3,2,1,0:T(8,128)(2,1)} %dft.2), channel_id=1, replica_groups=mesh['band'=4,'col'=8] {'col'}, dimensions={0} | all-to-all | bytes 6553600 | tf_op jit(solution)/shard_map/all_to_all | solution.py:140
  426.0 0.8 copy.20
  426.8 5.4 %fusion.14 = bf16[20,320,2,128]{3,1,2,0:T(8,128)(2,1)} fusion(f32[20,320]{1,0:T(8,128)S(1)} %get-tuple-element.7, bf16[320,2,20,128]{3,0,2,1:T(8,128)(2,1)S(1)} %bitcast.42, bf16[40,320,320]{2,1,0:T(8,128)(2,1)} %param.10), kind=kOutput, calls=%fused_computation.12 | convolution fusion | flops 1051852800 | bytes 11494400 | tf_op jit(solution)/shard_map/xpsl,sxn->snpl/dot_general | solution.py:142
  432.2 0.0 reduce-scatter.3.cloned.1.call-update
  432.2 0.0 reduce-scatter.5.cloned.1.call-done
  432.3 44.0 %reduce-scatter.3.cloned.1.call-done = bf16[20,80,2,128]{3,1,2,0:T(8,128)(2,1)} async-done(((bf16[20,320,2,128]{3,1,2,0:T(8,128)(2,1)}), bf16[20,80,2,128]{3,1,2,0:T(8,128)(2,1)}) %reduce-scatter.3.cloned.1.call-update) | async-done | bytes 819216 | tf_op jit(solution)/shard_map/reduce_scatter | solution.py:153
  476.3 1.6 maximum_convert_fusion
  477.9 3.4 copy.28
  (13 shorter events, 0.0 us)
Async XLA Ops:
  6.5 205.3 %copy-start = (s32[3,2]{0,1:T(2,128)S(1)}, s32[3,2]{0,1:T(2,128)}, u32[]{:S(2)}) copy-start(s32[3,2]{0,1:T(2,128)} %param.15) | copy-start | bytes 76
  26.9 6.5 %copy-start.2 = (s32[320]{0:T(512)S(1)}, s32[320]{0:T(512)}, u32[]{:S(2)}) copy-start(s32[320]{0:T(512)} %param.13) | copy-start | bytes 3844
  26.9 151.1 %all-to-all-start = ((bf16[8,40,80,128]{3,2,1,0:T(8,128)(2,1)}), bf16[8,40,80,128]{3,2,1,0:T(8,128)(2,1)}, u32[]{:S(2)}, u32[]{:S(2)}) async-start(bf16[8,40,80,128]{3,2,1,0:T(8,128)(2,1)} %bitcast.40), calls=%async_computation | async-start | bytes 13107200 | tf_op jit(solution)/shard_map/all_to_all | solution.py:119
  207.2 103.8 %all-to-all-start.2 = ((bf16[8,40,40,128]{3,2,1,0:T(8,128)(2,1)}), bf16[8,40,40,128]{3,2,1,0:T(8,128)(2,1)S(1)}, u32[]{:S(2)}, u32[]{:S(2)}) async-start(bf16[8,40,40,128]{3,2,1,0:T(8,128)(2,1)} %dft.3), calls=%async_computation.3 | async-start | bytes 6553600 | tf_op jit(solution)/shard_map/all_to_all | solution.py:140
  210.9 221.4 %reduce-scatter.5.cloned.1.call-start = ((), (), s32[]{:S(2)}) async-start(), calls=%async_computation.6 | async-start | bytes 4096000 | tf_op jit(solution)/shard_map/reduce_scatter | solution.py:153
  317.3 159.0 %reduce-scatter.3.cloned.1.call-start = ((), (), s32[]{:S(2)}) async-start(), calls=%async_computation.5 | async-start | bytes 4096000 | tf_op jit(solution)/shard_map/reduce_scatter | solution.py:153
  432.2 49.0 %copy-start.1 = (s32[3,2]{0,1:T(2,128)S(1)}, s32[3,2]{0,1:T(2,128)}, u32[]{:S(2)}) copy-start(s32[3,2]{0,1:T(2,128)} %param.15) | copy-start | bytes 76
Sparse Core Ops, SparseCore 0:
  317.4 46.1 reduce-scatter.4
  432.3 43.8 reduce-scatter.2

commit v2 on v1

v2 whole, which is shorter than its diff:
```python
import math

import jax
import jax.numpy as jnp
from jax import lax
from jax.experimental import pallas as pl
from jax.experimental.pallas import tpu as pltpu
from jax.sharding import PartitionSpec as P

LVR = 112
CHUNKS = (2, 2, 1)


def weights_kernel(points_ref, wave_ref, part_ref, *out_refs):
    count = jnp.full((1, 1), points_ref[pl.program_id(0)], jnp.int32).astype(jnp.float32)
    lons = out_refs[0].shape[2]
    lon = lax.broadcasted_iota(jnp.int32, (1, lons), 1).astype(jnp.float32)
    full = 4.0 * count
    inverse = 1.0 / full
    unit = (2.0 * math.pi) * inverse
    scale = jnp.where(lon < count, lax.rsqrt(count), 0.0)
    nearest = 1.5 * 2.0**23
    first = 0
    for out_ref in out_refs:
        cols = out_ref.shape[1]
        tile = 8 if cols % 16 else 16

        def rows(k, carry, out_ref=out_ref, first=first, tile=tile):
            at = pl.multiple_of(k * tile, tile)
            wave = wave_ref[pl.ds(first + at, tile), :]
            shift = part_ref[pl.ds(first + at, tile), :] * count
            turns = wave * lon + shift
            whole = (turns * inverse + nearest) - nearest
            rest = turns - whole * full
            theta = (count - jnp.abs(rest)) * unit
            square = theta * theta
            value = -1.0 / 39916800.0 * square + 1.0 / 362880.0
            value = value * square - 1.0 / 5040.0
            value = value * square + 1.0 / 120.0
            value = value * square - 1.0 / 6.0
            value = value * square + 1.0
            value = value * (theta * scale)
            out_ref[0, pl.ds(at, tile), :] = value.astype(jnp.bfloat16)
            return carry

        lax.fori_loop(0, cols // tile, rows, 0)
        first += cols


def dft_weights(points, chunks, lon_count):
    lats = points.shape[0]
    wave, part, shapes = [], [], []
    for waves in chunks:
        owners, slots = waves.shape
        shape = (owners, 2, slots)
        wave.append(jnp.broadcast_to(4.0 * waves.astype(jnp.float32)[:, None], shape).reshape(-1))
        part.append(
            jnp.broadcast_to(jnp.arange(2, dtype=jnp.float32)[None, :, None], shape).reshape(-1)
        )
        shapes.append((lats, owners * 2 * slots, lon_count))
    wave = jnp.concatenate(wave)[:, None]
    part = jnp.concatenate(part)[:, None]
    cols = wave.shape[0]
    return pl.pallas_call(
        weights_kernel,
        grid_spec=pltpu.PrefetchScalarGridSpec(
            num_scalar_prefetch=1,
            grid=(lats,),
            in_specs=[pl.BlockSpec((cols, 1), lambda i, p: (0, 0))] * 2,
            out_specs=[pl.BlockSpec((1,) + sh[1:], lambda i, p: (i, 0, 0)) for sh in shapes],
        ),
        out_shape=[jax.ShapeDtypeStruct(sh, jnp.bfloat16) for sh in shapes],
        cost_estimate=pl.CostEstimate(
            flops=25 * lats * cols * lon_count,
            bytes_accessed=2 * lats * cols * lon_count,
            transcendentals=0,
        ),
        name="weights",
    )(points, wave, part)


def dft_kernel(weight_ref, grid_ref, out_ref):
    lons = grid_ref.shape[0] * grid_ref.shape[2]
    owners, _, rows, levels = out_ref.shape
    for i in range(grid_ref.shape[1]):
        column = grid_ref[:, i].reshape(lons, levels)
        result = jnp.dot(weight_ref[i], column, preferred_element_type=jnp.float32)
        out_ref[:, i] = result.astype(jnp.bfloat16).reshape(owners, rows, levels)


def dft(weights, grid_field, owners):
    lats, cols, lons = weights.shape
    ranks, _, lon_local, levels = grid_field.shape
    rows = cols // owners
    block = max(d for d in range(1, 9) if lats % d == 0)
    return pl.pallas_call(
        dft_kernel,
        grid=(lats // block,),
        in_specs=[
            pl.BlockSpec((block, cols, lons), lambda i: (i, 0, 0)),
            pl.BlockSpec((ranks, block, lon_local, levels), lambda i: (0, i, 0, 0)),
        ],
        out_specs=pl.BlockSpec((owners, block, rows, levels), lambda i: (0, i, 0, 0)),
        out_shape=jax.ShapeDtypeStruct((owners, lats, rows, levels), jnp.bfloat16),
        cost_estimate=pl.CostEstimate(
            flops=2 * lats * cols * lons * levels,
            bytes_accessed=2 * lats * (cols * lons + (cols + lons) * levels),
            transcendentals=0,
        ),
        name="dft",
    )(weights, grid_field)


def per_device(
    control, vertical_root, legendre, band_filter, row_plan, wave_order, lat_points, support
):
    owners = lax.axis_size("col")
    band_id = row_plan[0, 0]
    level_start = row_plan[0, 1]
    root_band = lax.dynamic_index_in_dim(vertical_root, band_id, 0, keepdims=False)
    level = jnp.arange(root_band.shape[1], dtype=jnp.int32)
    inside = (level >= level_start) & (level < level_start + LVR)
    root_block = jnp.where(inside[None, :], root_band, jnp.zeros_like(root_band))
    columns = control[0]
    lon_local, lat_count, _ = columns.shape
    rooted = jnp.einsum(
        "jik,kl->ijl", columns, root_block, preferred_element_type=jnp.float32
    ).astype(jnp.bfloat16)
    rooted = rooted.reshape(owners, lat_count // owners, lon_local, -1)
    grid_field = lax.all_to_all(rooted, "col", split_axis=0, concat_axis=0, tiled=True)
    lon_count = lon_local * owners
    lat_local = lat_count // owners

    slot_count = legendre.shape[0]
    degree_count = legendre.shape[2]
    ends = [slot_count * sum(CHUNKS[: c + 1]) // sum(CHUNKS) for c in range(len(CHUNKS))]
    spans = list(zip([0] + ends[:-1], ends))
    waves = wave_order.reshape(owners, slot_count)
    owned_waves = lax.dynamic_index_in_dim(waves, lax.axis_index("col"), 0, keepdims=False)
    degree = jnp.arange(degree_count, dtype=jnp.int32)
    bounds = lax.dynamic_index_in_dim(support, band_id, 0, keepdims=False)
    filter_row = lax.dynamic_index_in_dim(band_filter, band_id, 0, keepdims=False)
    window = filter_row * ((degree >= bounds[0]) & (degree < bounds[1])).astype(jnp.float32)

    weights = dft_weights(lat_points, [waves[:, lo:hi] for lo, hi in spans], lon_count)
    outputs = []
    fourier = dft(weights[0], grid_field, owners)
    for c, (lo, hi) in enumerate(spans):
        owned = lax.all_to_all(fourier, "col", split_axis=0, concat_axis=0, tiled=True)
        if c + 1 < len(spans):
            fourier = dft(weights[c + 1], grid_field, owners)
        if c:
            fourier, owned, _ = lax.optimization_barrier((fourier, owned, contribution))
        else:
            fourier, owned = lax.optimization_barrier((fourier, owned))
        owned = owned.reshape(lat_count, 2, hi - lo, owned.shape[3])
        spectral = jnp.einsum(
            "xpsl,sxn->snpl",
            owned,
            legendre[lo:hi],
            preferred_element_type=jnp.float32,
        )
        spectral_weight = (degree[None, :] >= owned_waves[lo:hi][:, None]).astype(
            jnp.float32
        ) * window[None, :]
        contribution = (spectral * spectral_weight[:, :, None, None]).astype(jnp.bfloat16)
        if c:
            contribution, outputs[-1] = lax.optimization_barrier((contribution, outputs[-1]))
        outputs.append(
            lax.psum_scatter(contribution, "band", scatter_dimension=1, tiled=True)
        )
    return jnp.concatenate(outputs, axis=0).astype(jnp.float32)


def solution(mesh):
    in_specs = (
        P("band", "col", None, None),
        P(),
        P("col", None, None),
        P(),
        P("band", None),
        P(),
        P("col"),
        P(),
    )
    out_specs = P("col", "band", None, None)
    return jax.shard_map(
        per_device, mesh=mesh, in_specs=in_specs, out_specs=out_specs, check_vma=False
    )
```

time: 490 us -> 447 us (0.912)
  blocking collectives: 79.1 us -> 0 us
  waiting for transfers between devices: 90.6 us -> 163 us
  Pallas kernels: 252 us -> 203 us
  starting transfers between devices: 10.4 us -> 19.1 us
  matrix products: 19.8 us -> 26.6 us
    all_to_all x1 -> x3, waiting for transfers between devices: 0.01 us -> 131 us  [per_device(): lax.all_to_all(fourier, 'col', split_axis=0, concat_axis=0, tiled=True)]
    all_to_all x1 -> x0, blocking collectives: 79.1 us -> none  [per_device(): lax.all_to_all(fourier, 'col', split_axis=0, concat_axis=0, tiled=True)]
    all_to_all x1, waiting for transfers between devices: 46.5 us -> 0.01 us  [per_device(): lax.all_to_all(rooted, 'col', split_axis=0, concat_axis=0, tiled=True)]
    pallas_call x2 -> x3, Pallas kernels: 58.7 us -> 28.8 us  [dft(): pl.pallas_call(dft_kernel, grid=(lats // block,), in_specs=[pl.BlockSpec(...]
    pallas_call x2 -> x1, Pallas kernels: 193 us -> 174 us  [dft_weights(): pl.pallas_call(weights_kernel, grid_spec=pltpu.PrefetchScalarGridSpec(num...]
    reduce_scatter x2 -> x3, waiting for transfers between devices: 44 us -> 31.6 us  [per_device(): lax.psum_scatter(contribution, 'band', scatter_dimension=1, tiled=True)]
    all_to_all x1 -> x3, starting transfers between devices: 3.66 us -> 12.3 us  [per_device(): lax.all_to_all(fourier, 'col', split_axis=0, concat_axis=0, tiled=True)]
    dot_general x2 -> x3, matrix products: 10.9 us -> 17.7 us  [per_device(): jnp.einsum('xpsl,sxn->snpl', owned, legendre[lo:hi], preferred_element_ty...]
  transfers between devices with their start and end apart: 4 -> 7, of which waited for: 2 -> 4; matrix products, arithmetic and copies ran while one was open for 2% -> 4% of each run, Pallas kernels for 46% -> 43%
where the time goes in v2:
time: 447 us; the launch traced here: 446 us
  Pallas kernels  203 us (45%)
  waiting for transfers between devices  163 us (36%)
  matrix products  26.6 us (6%)
  starting transfers between devices  19.1 us (4%)
  between operations  15.7 us (4%)
  local copies, waits for them, and re-layouts  14.8 us (3%)
    pallas_call x1, Pallas kernels, dft_weights(): pl.pallas_call(weights_kernel, grid_spec=pltpu.PrefetchScalarGridSpec(num...  174 us
    all_to_all x3, waiting for transfers between devices, per_device(): lax.all_to_all(fourier, 'col', split_axis=0, concat_axis=0, tiled=True)  131 us
    reduce_scatter x3, waiting for transfers between devices, per_device(): lax.psum_scatter(contribution, 'band', scatter_dimension=1, tiled=True)  31.6 us
    pallas_call x3, Pallas kernels, dft(): pl.pallas_call(dft_kernel, grid=(lats // block,), in_specs=[pl.BlockSpec(...  28.8 us
    dot_general x3, matrix products, per_device(): jnp.einsum('xpsl,sxn->snpl', owned, legendre[lo:hi], preferred_element_ty...  17.7 us
    all_to_all x3, starting transfers between devices, per_device(): lax.all_to_all(fourier, 'col', split_axis=0, concat_axis=0, tiled=True)  12.3 us
  transfers between devices with their start and end apart: 7, of which 4 were waited for; matrix products, arithmetic and copies ran while one was open for 4% of the time, Pallas kernels for 43%

profile of v2, /device:TPU:0, one launch (start us, length us, event | category | flops | bytes accessed | tf_op | source)
XLA Modules:
  0.0 446.0 jit_solution(17856401806111071002)
XLA Ops:
  6.5 1.3 fusion.47
  9.7 0.7 compare_and_fusion
  11.0 8.9 %fusion.5 = bf16[320,80,128]{2,0,1:T(8,128)(2,1)S(1)} fusion(bf16[80,320,137]{1,0,2:T(8,128)(2,1)} %bitcast.54, bf16[3,137,128]{2,1,0:T(8,128)(2,1)} %param.9, s32[]{:T(128)S(6)} %select_n.19, pred[128]{0:T(512)(128)(4,1)S(1)} %compare_and_fusion), kind=kOutput, calls=%fused_computation.3 | convolution fusion | flops 901137536 | bytes 15007876 | tf_op jit(solution)/shard_map/jik,kl->ijl/dot_general | solution.py:126
  19.9 6.9 %copy.21 = bf16[320,80,128]{2,1,0:T(8,128)(2,1)} copy(bf16[320,80,128]{2,0,1:T(8,128)(2,1)S(1)} %fusion.5) | data formatting | bytes 13107200 | tf_op jit(solution)/shard_map/convert_element_type | solution.py:128
  26.8 6.5 %all-to-all-start = ((bf16[8,40,80,128]{3,2,1,0:T(8,128)(2,1)}), bf16[8,40,80,128]{3,2,1,0:T(8,128)(2,1)}, u32[]{:S(2)}, u32[]{:S(2)}) async-start(bf16[8,40,80,128]{3,2,1,0:T(8,128)(2,1)} %bitcast.53), calls=%async_computation | async-start | bytes 13107200 | tf_op jit(solution)/shard_map/all_to_all | solution.py:130
  33.3 0.1 reshape.193
  33.5 0.1 reshape.196
  33.7 0.1 reshape.194
  33.8 0.1 reshape.195
  33.9 0.1 reshape.198
  34.0 0.1 reshape.197
  34.1 0.9 broadcast_in_dim.36.part_ref
  35.0 0.9 broadcast_in_dim.35.wave_ref
  35.8 174.0 %weights.1 = (bf16[40,256,640]{2,1,0:T(8,128)(2,1)}, bf16[40,256,640]{2,1,0:T(8,128)(2,1)}, bf16[40,128,640]{2,1,0:T(8,128)(2,1)}) custom-call(s32[40]{0:T(128)} %points_ref.1, f32[640,1]{1,0:T(8,128)} %broadcast_in_dim.35.wave_ref, f32[640,1]{1,0:T(8,128)} %broadcast_in_dim.36.part_ref), custom_call_target="tpu_custom_call" | custom-call | flops 409600000 | bytes 32768000 | tf_op jit(solution)/shard_map/weights/pallas_call | solution.py:64
  209.9 10.5 %dft.5 = bf16[8,40,32,128]{3,2,1,0:T(8,128)(2,1)} custom-call(bf16[40,256,640]{2,1,0:T(8,128)(2,1)} %get-tuple-element.19.weight_ref, bf16[8,40,80,128]{3,2,1,0:T(8,128)(2,1)} %all-to-all-done.grid_ref), custom_call_target="tpu_custom_call" | custom-call | flops 1677721600 | bytes 22282240 | tf_op jit(solution)/shard_map/dft/pallas_call | solution.py:96
  220.4 5.1 %all-to-all-start.1 = ((bf16[8,40,32,128]{3,2,1,0:T(8,128)(2,1)}), bf16[8,40,32,128]{3,2,1,0:T(8,128)(2,1)S(1)}, u32[]{:S(2)}, u32[]{:S(2)}) async-start(bf16[8,40,32,128]{3,2,1,0:T(8,128)(2,1)} %dft.5), calls=%async_computation.1 | async-start | bytes 5242880 | tf_op jit(solution)/shard_map/all_to_all | solution.py:149
  225.5 0.2 reduce-scatter.4.cloned.1.call-start
  225.8 0.6 fusion.46
  226.4 2.0 fusion.43
  228.6 10.5 %dft.4 = bf16[8,40,32,128]{3,2,1,0:T(8,128)(2,1)} custom-call(bf16[40,256,640]{2,1,0:T(8,128)(2,1)} %get-tuple-element.18.weight_ref, bf16[8,40,80,128]{3,2,1,0:T(8,128)(2,1)} %all-to-all-done.grid_ref), custom_call_target="tpu_custom_call" | custom-call | flops 1677721600 | bytes 22282240 | tf_op jit(solution)/shard_map/dft/pallas_call | solution.py:96
  239.0 46.7 %all-to-all-done.1 = bf16[8,40,32,128]{3,2,1,0:T(8,128)(2,1)S(1)} async-done(((bf16[8,40,32,128]{3,2,1,0:T(8,128)(2,1)}), bf16[8,40,32,128]{3,2,1,0:T(8,128)(2,1)S(1)}, u32[]{:S(2)}, u32[]{:S(2)}) %all-to-all-start.1) | async-done | bytes 2621472 | tf_op jit(solution)/shard_map/all_to_all | solution.py:149
  285.7 7.0 %fusion.14 = bf16[16,320,2,128]{3,1,2,0:T(8,128)(2,1)} fusion(f32[16,320]{1,0:T(8,128)S(1)} %get-tuple-element.32, bf16[320,2,16,128]{3,2,1,0:T(8,128)(2,1)S(1)} %bitcast.55, bf16[40,320,320]{2,1,0:T(8,128)(2,1)} %param.10), kind=kOutput, calls=%fused_computation.12 | convolution fusion | flops 841482240 | bytes 9195520 | tf_op jit(solution)/shard_map/xpsl,sxn->snpl/dot_general | solution.py:157
  292.7 3.6 all-to-all-start.2
  296.4 7.9 %dft.3 = bf16[8,40,16,128]{3,2,1,0:T(8,128)(2,1)} custom-call(bf16[40,128,640]{2,1,0:T(8,128)(2,1)} %get-tuple-element.17.weight_ref, bf16[8,40,80,128]{3,2,1,0:T(8,128)(2,1)} %all-to-all-done.grid_ref), custom_call_target="tpu_custom_call" | custom-call | flops 838860800 | bytes 14417920 | tf_op jit(solution)/shard_map/dft/pallas_call | solution.py:96
  304.3 52.3 %all-to-all-done.2 = bf16[8,40,32,128]{3,2,1,0:T(8,128)(2,1)S(1)} async-done(((bf16[8,40,32,128]{3,2,1,0:T(8,128)(2,1)}), bf16[8,40,32,128]{3,2,1,0:T(8,128)(2,1)S(1)}, u32[]{:S(2)}, u32[]{:S(2)}) %all-to-all-start.2) | async-done | bytes 2621472 | tf_op jit(solution)/shard_map/all_to_all | solution.py:149
  356.6 7.0 %fusion.15 = bf16[16,320,2,128]{3,1,2,0:T(8,128)(2,1)} fusion(f32[16,320]{1,0:T(8,128)S(1)} %get-tuple-element.31, bf16[320,2,16,128]{3,2,1,0:T(8,128)(2,1)S(1)} %bitcast.56, bf16[40,320,320]{2,1,0:T(8,128)(2,1)} %param.10), kind=kOutput, calls=%fused_computation.13 | convolution fusion | flops 841482240 | bytes 9195520 | tf_op jit(solution)/shard_map/xpsl,sxn->snpl/dot_general | solution.py:157
  363.5 3.6 all-to-all-start.3
  367.3 31.9 %all-to-all-done.3 = bf16[8,40,16,128]{3,2,1,0:T(8,128)(2,1)S(1)} async-done(((bf16[8,40,16,128]{3,2,1,0:T(8,128)(2,1)}), bf16[8,40,16,128]{3,2,1,0:T(8,128)(2,1)S(1)}, u32[]{:S(2)}, u32[]{:S(2)}) %all-to-all-start.3) | async-done | bytes 1310752 | tf_op jit(solution)/shard_map/all_to_all | solution.py:149
  399.2 3.8 fusion.31
  403.0 31.6 %reduce-scatter.8.cloned.1.call-done = bf16[8,80,2,128]{3,1,2,0:T(8,128)(2,1)} async-done(((bf16[8,320,2,128]{3,1,2,0:T(8,128)(2,1)}), bf16[8,80,2,128]{3,1,2,0:T(8,128)(2,1)}) %reduce-scatter.8.cloned.1.call-update) | async-done | bytes 327696 | tf_op jit(solution)/shard_map/reduce_scatter | solution.py:170
  434.6 1.4 maximum_convert_fusion
  436.1 3.4 copy.28
  (31 shorter events, 0.7 us)
Async XLA Ops:
  6.5 219.2 %copy-start = (s32[3,2]{0,1:T(2,128)S(1)}, s32[3,2]{0,1:T(2,128)}, u32[]{:S(2)}) copy-start(s32[3,2]{0,1:T(2,128)} %param.15) | copy-start | bytes 76
  26.8 6.5 %copy-start.3 = (s32[320]{0:T(512)S(1)}, s32[320]{0:T(512)}, u32[]{:S(2)}) copy-start(s32[320]{0:T(512)} %param.13) | copy-start | bytes 3844
  26.8 183.0 %all-to-all-start = ((bf16[8,40,80,128]{3,2,1,0:T(8,128)(2,1)}), bf16[8,40,80,128]{3,2,1,0:T(8,128)(2,1)}, u32[]{:S(2)}, u32[]{:S(2)}) async-start(bf16[8,40,80,128]{3,2,1,0:T(8,128)(2,1)} %bitcast.53), calls=%async_computation | async-start | bytes 13107200 | tf_op jit(solution)/shard_map/all_to_all | solution.py:130
  220.4 65.4 %all-to-all-start.1 = ((bf16[8,40,32,128]{3,2,1,0:T(8,128)(2,1)}), bf16[8,40,32,128]{3,2,1,0:T(8,128)(2,1)S(1)}, u32[]{:S(2)}, u32[]{:S(2)}) async-start(bf16[8,40,32,128]{3,2,1,0:T(8,128)(2,1)} %dft.5), calls=%async_computation.1 | async-start | bytes 5242880 | tf_op jit(solution)/shard_map/all_to_all | solution.py:149
  225.5 138.1 %reduce-scatter.4.cloned.1.call-start = ((), (), s32[]{:S(2)}) async-start(), calls=%async_computation.7 | async-start | bytes 3276800 | tf_op jit(solution)/shard_map/reduce_scatter | solution.py:170
  292.7 63.8 %all-to-all-start.2 = ((bf16[8,40,32,128]{3,2,1,0:T(8,128)(2,1)}), bf16[8,40,32,128]{3,2,1,0:T(8,128)(2,1)S(1)}, u32[]{:S(2)}, u32[]{:S(2)}) async-start(bf16[8,40,32,128]{3,2,1,0:T(8,128)(2,1)} %dft.4), calls=%async_computation.2 | async-start | bytes 5242880 | tf_op jit(solution)/shard_map/all_to_all | solution.py:149
  296.4 106.7 %reduce-scatter.6.cloned.1.call-start = ((), (), s32[]{:S(2)}) async-start(), calls=%async_computation.8 | async-start | bytes 3276800 | tf_op jit(solution)/shard_map/reduce_scatter | solution.py:170
  363.5 35.7 %all-to-all-start.3 = ((bf16[8,40,16,128]{3,2,1,0:T(8,128)(2,1)}), bf16[8,40,16,128]{3,2,1,0:T(8,128)(2,1)S(1)}, u32[]{:S(2)}, u32[]{:S(2)}) async-start(bf16[8,40,16,128]{3,2,1,0:T(8,128)(2,1)} %dft.3), calls=%async_computation.4 | async-start | bytes 2621440 | tf_op jit(solution)/shard_map/all_to_all | solution.py:149
  367.1 67.5 %reduce-scatter.8.cloned.1.call-start = ((), (), s32[]{:S(2)}) async-start(), calls=%async_computation.9 | async-start | bytes 1638400 | tf_op jit(solution)/shard_map/reduce_scatter | solution.py:170
  399.2 35.4 %copy-start.2 = (bf16[16,80,2,128]{3,1,2,0:T(8,128)(2,1)S(1)}, bf16[16,80,2,128]{3,1,2,0:T(8,128)(2,1)}, u32[]{:S(2)}) copy-start(bf16[16,80,2,128]{3,1,2,0:T(8,128)(2,1)} %reduce-scatter.4.cloned.1.call-done) | copy-start | bytes 1966084
  434.6 4.8 %copy-start.1 = (s32[3,2]{0,1:T(2,128)S(1)}, s32[3,2]{0,1:T(2,128)}, u32[]{:S(2)}) copy-start(s32[3,2]{0,1:T(2,128)} %param.15) | copy-start | bytes 76
Sparse Core Ops, SparseCore 0:
  292.8 38.4 reduce-scatter.3
  363.7 38.4 reduce-scatter.5
  405.1 29.4 reduce-scatter.7

commit v3 on v2

--- a/solution.py
+++ b/solution.py
@@ -11,9 +11,20 @@
 CHUNKS = (2, 2, 1)
 
 
-def weights_kernel(points_ref, wave_ref, part_ref, *out_refs):
+def sine(theta):
+    square = theta * theta
+    value = -1.0 / 39916800.0 * square + 1.0 / 362880.0
+    value = value * square - 1.0 / 5040.0
+    value = value * square + 1.0 / 120.0
+    value = value * square - 1.0 / 6.0
+    value = value * square + 1.0
+    return value * theta
+
+
+def weights_kernel(points_ref, wave_ref, *out_refs):
     count = jnp.full((1, 1), points_ref[pl.program_id(0)], jnp.int32).astype(jnp.float32)
     lons = out_refs[0].shape[2]
+    lanes = 128
     lon = lax.broadcasted_iota(jnp.int32, (1, lons), 1).astype(jnp.float32)
     full = 4.0 * count
     inverse = 1.0 / full
@@ -22,76 +33,80 @@
     nearest = 1.5 * 2.0**23
     first = 0
     for out_ref in out_refs:
-        cols = out_ref.shape[1]
-        tile = 8 if cols % 16 else 16
-
-        def rows(k, carry, out_ref=out_ref, first=first, tile=tile):
+        half = out_ref.shape[1] // 2
+        tile = 8 if half % 16 else 16
+
+        def rows(k, carry, out_ref=out_ref, first=first, tile=tile, half=half):
             at = pl.multiple_of(k * tile, tile)
-            wave = wave_ref[pl.ds(first + at, tile), :]
-            shift = part_ref[pl.ds(first + at, tile), :] * count
-            turns = wave * lon + shift
+            turns = wave_ref[pl.ds(first + at, tile), :] * lon[:, :lanes]
             whole = (turns * inverse + nearest) - nearest
             rest = turns - whole * full
-            theta = (count - jnp.abs(rest)) * unit
-            square = theta * theta
-            value = -1.0 / 39916800.0 * square + 1.0 / 362880.0
-            value = value * square - 1.0 / 5040.0
-            value = value * square + 1.0 / 120.0
-            value = value * square - 1.0 / 6.0
-            value = value * square + 1.0
-            value = value * (theta * scale)
-            out_ref[0, pl.ds(at, tile), :] = value.astype(jnp.bfloat16)
+            cos = sine((count - jnp.abs(rest)) * unit)
+            away = jnp.abs(rest - count)
+            sin = sine((count - jnp.minimum(away, full - away)) * unit)
+            middle = lanes // 2
+            cos_half = jnp.broadcast_to(cos[:, middle : middle + 1], cos.shape)
+            sin_half = jnp.broadcast_to(sin[:, middle : middle + 1], sin.shape)
+            cos_step = cos_half * cos_half - sin_half * sin_half
+            sin_step = 2.0 * (cos_half * sin_half)
+            for lo in range(0, lons, lanes):
+                if lo:
+                    cos, sin = (
+                        cos * cos_step - sin * sin_step,
+                        sin * cos_step + cos * sin_step,
+                    )
+                part = scale[:, lo : lo + lanes]
+                out_ref[0, pl.ds(at, tile), lo : lo + lanes] = (cos * part).astype(
+                    jnp.bfloat16
+                )
+                out_ref[0, pl.ds(half + at, tile), lo : lo + lanes] = (-sin * part).astype(
+                    jnp.bfloat16
+                )
             return carry
 
-        lax.fori_loop(0, cols // tile, rows, 0)
-        first += cols
+        lax.fori_loop(0, half // tile, rows, 0)
+        first += half
 
 
 def dft_weights(points, chunks, lon_count):
     lats = points.shape[0]
-    wave, part, shapes = [], [], []
-    for waves in chunks:
-        owners, slots = waves.shape
-        shape = (owners, 2, slots)
-        wave.append(jnp.broadcast_to(4.0 * waves.astype(jnp.float32)[:, None], shape).reshape(-1))
-        part.append(
-            jnp.broadcast_to(jnp.arange(2, dtype=jnp.float32)[None, :, None], shape).reshape(-1)
-        )
-        shapes.append((lats, owners * 2 * slots, lon_count))
-    wave = jnp.concatenate(wave)[:, None]
-    part = jnp.concatenate(part)[:, None]
-    cols = wave.shape[0]
+    shapes = [(lats, 2 * waves.size, lon_count) for waves in chunks]
+    wave = jnp.concatenate([waves.reshape(-1) for waves in chunks])
+    wave = 4.0 * wave.astype(jnp.float32)[:, None]
     return pl.pallas_call(
         weights_kernel,
         grid_spec=pltpu.PrefetchScalarGridSpec(
             num_scalar_prefetch=1,
             grid=(lats,),
-            in_specs=[pl.BlockSpec((cols, 1), lambda i, p: (0, 0))] * 2,
+            in_specs=[pl.BlockSpec(wave.shape, lambda i, p: (0, 0))],
             out_specs=[pl.BlockSpec((1,) + sh[1:], lambda i, p: (i, 0, 0)) for sh in shapes],
         ),
         out_shape=[jax.ShapeDtypeStruct(sh, jnp.bfloat16) for sh in shapes],
         cost_estimate=pl.CostEstimate(
-            flops=25 * lats * cols * lon_count,
-            bytes_accessed=2 * lats * cols * lon_count,
+            flops=20 * lats * wave.shape[0] * lon_count,
+            bytes_accessed=4 * lats * wave.shape[0] * lon_count,
             transcendentals=0,
         ),
         name="weights",
-    )(points, wave, part)
+    )(points, wave)
 
 
 def dft_kernel(weight_ref, grid_ref, out_ref):
     lons = grid_ref.shape[0] * grid_ref.shape[2]
-    owners, _, rows, levels = out_ref.shape
+    owners, _, parts, slots, levels = out_ref.shape
+    half = owners * slots
     for i in range(grid_ref.shape[1]):
         column = grid_ref[:, i].reshape(lons, levels)
         result = jnp.dot(weight_ref[i], column, preferred_element_type=jnp.float32)
-        out_ref[:, i] = result.astype(jnp.bfloat16).reshape(owners, rows, levels)
+        for p in range(parts):
+            piece = result[p * half : (p + 1) * half].reshape(owners, slots, levels)
+            out_ref[:, i, p] = piece.astype(jnp.bfloat16)
 
 
 def dft(weights, grid_field, owners):
     lats, cols, lons = weights.shape
     ranks, _, lon_local, levels = grid_field.shape
-    rows = cols // owners
+    slots = cols // (2 * owners)
     block = max(d for d in range(1, 9) if lats % d == 0)
     return pl.pallas_call(
         dft_kernel,
@@ -100,8 +115,8 @@
             pl.BlockSpec((block, cols, lons), lambda i: (i, 0, 0)),
             pl.BlockSpec((ranks, block, lon_local, levels), lambda i: (0, i, 0, 0)),
         ],
-        out_specs=pl.BlockSpec((owners, block, rows, levels), lambda i: (0, i, 0, 0)),
-        out_shape=jax.ShapeDtypeStruct((owners, lats, rows, levels), jnp.bfloat16),
+        out_specs=pl.BlockSpec((owners, block, 2, slots, levels), lambda i: (0, i, 0, 0, 0)),
+        out_shape=jax.ShapeDtypeStruct((owners, lats, 2, slots, levels), jnp.bfloat16),
         cost_estimate=pl.CostEstimate(
             flops=2 * lats * cols * lons * levels,
             bytes_accessed=2 * lats * (cols * lons + (cols + lons) * levels),
@@ -153,7 +168,7 @@
             fourier, owned, _ = lax.optimization_barrier((fourier, owned, contribution))
         else:
             fourier, owned = lax.optimization_barrier((fourier, owned))
-        owned = owned.reshape(lat_count, 2, hi - lo, owned.shape[3])
+        owned = owned.reshape(lat_count, 2, hi - lo, owned.shape[4])
         spectral = jnp.einsum(
             "xpsl,sxn->snpl",
             owned,

time: 447 us -> 420 us (0.940)
  Pallas kernels: 203 us -> 177 us
    pallas_call x1, Pallas kernels: 174 us -> 148 us  [dft_weights(): pl.pallas_call(weights_kernel, grid_spec=pltpu.PrefetchScalarGridSpec(num...]
  transfers between devices with their start and end apart: 7 -> 7, of which waited for: 4 -> 4; matrix products, arithmetic and copies ran while one was open for 4% -> 4% of each run, Pallas kernels for 43% -> 40%
where the time goes in v3:
time: 420 us; the launch traced here: 419 us
  Pallas kernels  177 us (42%)
  waiting for transfers between devices  163 us (39%)
  matrix products  26.6 us (6%)
  starting transfers between devices  19.1 us (5%)
  between operations  15.7 us (4%)
  local copies, waits for them, and re-layouts  13 us (3%)
  other arithmetic  4.97 us (1%)
    pallas_call x1, Pallas kernels, dft_weights(): pl.pallas_call(weights_kernel, grid_spec=pltpu.PrefetchScalarGridSpec(num...  148 us
    all_to_all x3, waiting for transfers between devices, per_device(): lax.all_to_all(fourier, 'col', split_axis=0, concat_axis=0, tiled=True)  131 us
    reduce_scatter x3, waiting for transfers between devices, per_device(): lax.psum_scatter(contribution, 'band', scatter_dimension=1, tiled=True)  31.6 us
    pallas_call x3, Pallas kernels, dft(): pl.pallas_call(dft_kernel, grid=(lats // block,), in_specs=[pl.BlockSpec(...  28.8 us
    dot_general x3, matrix products, per_device(): jnp.einsum('xpsl,sxn->snpl', owned, legendre[lo:hi], preferred_element_ty...  17.7 us
    all_to_all x3, starting transfers between devices, per_device(): lax.all_to_all(fourier, 'col', split_axis=0, concat_axis=0, tiled=True)  12.3 us
    dot_general x1, matrix products, per_device(): jnp.einsum('jik,kl->ijl', columns, root_block, preferred_element_type=jnp...  8.91 us
  transfers between devices with their start and end apart: 7, of which 4 were waited for; matrix products, arithmetic and copies ran while one was open for 4% of the time, Pallas kernels for 40%

profile of v3, /device:TPU:0, one launch (start us, length us, event | category | flops | bytes accessed | tf_op | source)
XLA Modules:
  0.0 418.9 jit_solution(4185102400822356666)
XLA Ops:
  6.5 1.3 fusion.48
  9.7 0.7 compare_and_fusion
  11.0 8.9 %fusion.5 = bf16[320,80,128]{2,0,1:T(8,128)(2,1)S(1)} fusion(bf16[80,320,137]{1,0,2:T(8,128)(2,1)} %bitcast.54, bf16[3,137,128]{2,1,0:T(8,128)(2,1)} %param.9, s32[]{:T(128)S(6)} %select_n.19, pred[128]{0:T(512)(128)(4,1)S(1)} %compare_and_fusion), kind=kOutput, calls=%fused_computation.3 | convolution fusion | flops 901137536 | bytes 15007876 | tf_op jit(solution)/shard_map/jik,kl->ijl/dot_general | solution.py:141
  19.9 6.9 %copy.34 = bf16[320,80,128]{2,1,0:T(8,128)(2,1)} copy(bf16[320,80,128]{2,0,1:T(8,128)(2,1)S(1)} %fusion.5) | data formatting | bytes 13107200 | tf_op jit(solution)/shard_map/convert_element_type | solution.py:143
  26.8 6.5 %all-to-all-start = ((bf16[8,40,80,128]{3,2,1,0:T(8,128)(2,1)}), bf16[8,40,80,128]{3,2,1,0:T(8,128)(2,1)}, u32[]{:S(2)}, u32[]{:S(2)}) async-start(bf16[8,40,80,128]{3,2,1,0:T(8,128)(2,1)} %bitcast.53), calls=%async_computation | async-start | bytes 13107200 | tf_op jit(solution)/shard_map/all_to_all | solution.py:145
  33.3 0.1 reshape.221
  33.5 0.1 concatenate.21
  33.6 0.1 concatenate.19
  33.7 0.1 concatenate.20
  33.8 0.1 copy.31
  34.0 0.7 broadcast_multiply_fusion.wave_ref
  34.6 148.1 %weights.1 = (bf16[40,256,640]{2,1,0:T(8,128)(2,1)}, bf16[40,256,640]{2,1,0:T(8,128)(2,1)}, bf16[40,128,640]{2,1,0:T(8,128)(2,1)}) custom-call(s32[40]{0:T(128)} %points_ref.1, f32[320,1]{1,0:T(8,128)} %broadcast_multiply_fusion.wave_ref), custom_call_target="tpu_custom_call" | custom-call | flops 163840000 | bytes 32768000 | tf_op jit(solution)/shard_map/weights/pallas_call | solution.py:76
  182.7 10.5 %dft.5 = bf16[8,40,2,16,128]{4,3,2,1,0:T(8,128)(2,1)} custom-call(bf16[40,256,640]{2,1,0:T(8,128)(2,1)} %get-tuple-element.19.weight_ref, bf16[8,40,80,128]{3,2,1,0:T(8,128)(2,1)} %all-to-all-done.grid_ref), custom_call_target="tpu_custom_call" | custom-call | flops 1677721600 | bytes 22282240 | tf_op jit(solution)/shard_map/dft/pallas_call | solution.py:111
  193.2 5.1 %all-to-all-start.1 = ((bf16[8,40,2,16,128]{4,3,2,1,0:T(8,128)(2,1)}), bf16[8,40,2,16,128]{4,3,2,1,0:T(8,128)(2,1)S(1)}, u32[]{:S(2)}, u32[]{:S(2)}) async-start(bf16[8,40,2,16,128]{4,3,2,1,0:T(8,128)(2,1)} %dft.5), calls=%async_computation.1 | async-start | bytes 5242880 | tf_op jit(solution)/shard_map/all_to_all | solution.py:164
  198.3 0.2 reduce-scatter.4.cloned.1.call-start
  198.6 0.1 constant_dynamic-slice_fusion
  198.6 0.6 fusion.47
  199.2 2.0 fusion.43
  201.4 0.1 fusion.40
  201.4 10.5 %dft.4 = bf16[8,40,2,16,128]{4,3,2,1,0:T(8,128)(2,1)} custom-call(bf16[40,256,640]{2,1,0:T(8,128)(2,1)} %get-tuple-element.18.weight_ref, bf16[8,40,80,128]{3,2,1,0:T(8,128)(2,1)} %all-to-all-done.grid_ref), custom_call_target="tpu_custom_call" | custom-call | flops 1677721600 | bytes 22282240 | tf_op jit(solution)/shard_map/dft/pallas_call | solution.py:111
  211.9 46.7 %all-to-all-done.1 = bf16[8,40,2,16,128]{4,3,2,1,0:T(8,128)(2,1)S(1)} async-done(((bf16[8,40,2,16,128]{4,3,2,1,0:T(8,128)(2,1)}), bf16[8,40,2,16,128]{4,3,2,1,0:T(8,128)(2,1)S(1)}, u32[]{:S(2)}, u32[]{:S(2)}) %all-to-all-start.1) | async-done | bytes 2621472 | tf_op jit(solution)/shard_map/all_to_all | solution.py:164
  258.6 7.0 %fusion.14 = bf16[16,320,2,128]{3,1,2,0:T(8,128)(2,1)} fusion(f32[16,320]{1,0:T(8,128)S(1)} %get-tuple-element.32, bf16[320,2,16,128]{3,2,1,0:T(8,128)(2,1)S(1)} %bitcast.55, bf16[40,320,320]{2,1,0:T(8,128)(2,1)} %param.10), kind=kOutput, calls=%fused_computation.12 | convolution fusion | flops 841482240 | bytes 9195520 | tf_op jit(solution)/shard_map/xpsl,sxn->snpl/dot_general | solution.py:172
  265.6 3.6 all-to-all-start.2
  269.3 7.9 %dft.3 = bf16[8,40,2,8,128]{4,3,2,1,0:T(8,128)(2,1)} custom-call(bf16[40,128,640]{2,1,0:T(8,128)(2,1)} %get-tuple-element.17.weight_ref, bf16[8,40,80,128]{3,2,1,0:T(8,128)(2,1)} %all-to-all-done.grid_ref), custom_call_target="tpu_custom_call" | custom-call | flops 838860800 | bytes 14417920 | tf_op jit(solution)/shard_map/dft/pallas_call | solution.py:111
  277.2 52.3 %all-to-all-done.2 = bf16[8,40,2,16,128]{4,3,2,1,0:T(8,128)(2,1)S(1)} async-done(((bf16[8,40,2,16,128]{4,3,2,1,0:T(8,128)(2,1)}), bf16[8,40,2,16,128]{4,3,2,1,0:T(8,128)(2,1)S(1)}, u32[]{:S(2)}, u32[]{:S(2)}) %all-to-all-start.2) | async-done | bytes 2621472 | tf_op jit(solution)/shard_map/all_to_all | solution.py:164
  329.4 7.0 %fusion.15 = bf16[16,320,2,128]{3,1,2,0:T(8,128)(2,1)} fusion(f32[16,320]{1,0:T(8,128)S(1)} %get-tuple-element.31, bf16[320,2,16,128]{3,2,1,0:T(8,128)(2,1)S(1)} %bitcast.56, bf16[40,320,320]{2,1,0:T(8,128)(2,1)} %param.10), kind=kOutput, calls=%fused_computation.13 | convolution fusion | flops 841482240 | bytes 9195520 | tf_op jit(solution)/shard_map/xpsl,sxn->snpl/dot_general | solution.py:172
  336.4 3.6 all-to-all-start.3
  340.2 31.9 %all-to-all-done.3 = bf16[8,40,2,8,128]{4,3,2,1,0:T(8,128)(2,1)S(1)} async-done(((bf16[8,40,2,8,128]{4,3,2,1,0:T(8,128)(2,1)}), bf16[8,40,2,8,128]{4,3,2,1,0:T(8,128)(2,1)S(1)}, u32[]{:S(2)}, u32[]{:S(2)}) %all-to-all-start.3) | async-done | bytes 1310752 | tf_op jit(solution)/shard_map/all_to_all | solution.py:164
  372.1 3.8 fusion.31
  375.9 31.6 %reduce-scatter.8.cloned.1.call-done = bf16[8,80,2,128]{3,1,2,0:T(8,128)(2,1)} async-done(((bf16[8,320,2,128]{3,1,2,0:T(8,128)(2,1)}), bf16[8,80,2,128]{3,1,2,0:T(8,128)(2,1)}) %reduce-scatter.8.cloned.1.call-update) | async-done | bytes 327696 | tf_op jit(solution)/shard_map/reduce_scatter | solution.py:185
  407.5 1.4 maximum_convert_fusion
  408.9 3.4 copy.41
  (23 shorter events, 0.5 us)
Async XLA Ops:
  6.5 192.0 %copy-start = (s32[3,2]{0,1:T(2,128)S(1)}, s32[3,2]{0,1:T(2,128)}, u32[]{:S(2)}) copy-start(s32[3,2]{0,1:T(2,128)} %param.15) | copy-start | bytes 76
  26.8 6.5 %copy-start.3 = (s32[320]{0:T(512)S(1)}, s32[320]{0:T(512)}, u32[]{:S(2)}) copy-start(s32[320]{0:T(512)} %param.13) | copy-start | bytes 3844
  26.8 155.9 %all-to-all-start = ((bf16[8,40,80,128]{3,2,1,0:T(8,128)(2,1)}), bf16[8,40,80,128]{3,2,1,0:T(8,128)(2,1)}, u32[]{:S(2)}, u32[]{:S(2)}) async-start(bf16[8,40,80,128]{3,2,1,0:T(8,128)(2,1)} %bitcast.53), calls=%async_computation | async-start | bytes 13107200 | tf_op jit(solution)/shard_map/all_to_all | solution.py:145
  193.2 65.4 %all-to-all-start.1 = ((bf16[8,40,2,16,128]{4,3,2,1,0:T(8,128)(2,1)}), bf16[8,40,2,16,128]{4,3,2,1,0:T(8,128)(2,1)S(1)}, u32[]{:S(2)}, u32[]{:S(2)}) async-start(bf16[8,40,2,16,128]{4,3,2,1,0:T(8,128)(2,1)} %dft.5), calls=%async_computation.1 | async-start | bytes 5242880 | tf_op jit(solution)/shard_map/all_to_all | solution.py:164
  198.3 138.1 %reduce-scatter.4.cloned.1.call-start = ((), (), s32[]{:S(2)}) async-start(), calls=%async_computation.7 | async-start | bytes 3276800 | tf_op jit(solution)/shard_map/reduce_scatter | solution.py:185
  265.6 63.8 %all-to-all-start.2 = ((bf16[8,40,2,16,128]{4,3,2,1,0:T(8,128)(2,1)}), bf16[8,40,2,16,128]{4,3,2,1,0:T(8,128)(2,1)S(1)}, u32[]{:S(2)}, u32[]{:S(2)}) async-start(bf16[8,40,2,16,128]{4,3,2,1,0:T(8,128)(2,1)} %dft.4), calls=%async_computation.2 | async-start | bytes 5242880 | tf_op jit(solution)/shard_map/all_to_all | solution.py:164
  269.2 106.7 %reduce-scatter.6.cloned.1.call-start = ((), (), s32[]{:S(2)}) async-start(), calls=%async_computation.8 | async-start | bytes 3276800 | tf_op jit(solution)/shard_map/reduce_scatter | solution.py:185
  336.4 35.7 %all-to-all-start.3 = ((bf16[8,40,2,8,128]{4,3,2,1,0:T(8,128)(2,1)}), bf16[8,40,2,8,128]{4,3,2,1,0:T(8,128)(2,1)S(1)}, u32[]{:S(2)}, u32[]{:S(2)}) async-start(bf16[8,40,2,8,128]{4,3,2,1,0:T(8,128)(2,1)} %dft.3), calls=%async_computation.4 | async-start | bytes 2621440 | tf_op jit(solution)/shard_map/all_to_all | solution.py:164
  340.0 67.5 %reduce-scatter.8.cloned.1.call-start = ((), (), s32[]{:S(2)}) async-start(), calls=%async_computation.9 | async-start | bytes 1638400 | tf_op jit(solution)/shard_map/reduce_scatter | solution.py:185
  372.1 35.4 %copy-start.2 = (bf16[16,80,2,128]{3,1,2,0:T(8,128)(2,1)S(1)}, bf16[16,80,2,128]{3,1,2,0:T(8,128)(2,1)}, u32[]{:S(2)}) copy-start(bf16[16,80,2,128]{3,1,2,0:T(8,128)(2,1)} %reduce-scatter.4.cloned.1.call-done) | copy-start | bytes 1966084
  407.5 4.8 %copy-start.1 = (s32[3,2]{0,1:T(2,128)S(1)}, s32[3,2]{0,1:T(2,128)}, u32[]{:S(2)}) copy-start(s32[3,2]{0,1:T(2,128)} %param.15) | copy-start | bytes 76
Sparse Core Ops, SparseCore 0:
  265.7 38.4 reduce-scatter.3
  336.5 38.4 reduce-scatter.5
  378.0 29.4 reduce-scatter.7
